TPU v7x, 512 devices: a whole 4x8x8 slice. The times are simulated.
512 devices in a mesh: tm: 256 (over z, y, x), state: 2 (over core).
Axes of the slice: x: 4, y: 8, z: 8, core: 2. Of those that a mesh axis runs over, the one named last changes fastest.
Arguments:
- features: float32 [4, 4096, 512], P(None, 'tm'), may hold values from -18 to 18
- gauss_means: float32 [1024, 512], P('state'), may hold values from -3 to 3
- precisions: float32 [1024, 512], P('state'), may hold values from 0.5 to 2
- transitions: bfloat16 [1024, 1024], P('state'), may hold values from 0 to 1, as said below
- initial: bfloat16 [1024], P('state'), may hold values from 0.099609375 to 10
- reset_flags: int32 [4, 4096], P(None, 'tm'), may hold values from 0 to 1, as said below
Outputs:
- posteriors: bfloat16 [4, 4096, 1024], P(None, 'tm', 'state')
- evidence: float32 [4, 4096], P(None, ('tm', 'state'))
Inputs may be any that keep to these rules, and one draw needn't show every extreme that they name: `transitions`: every entry nonnegative; each row sums to 1 up to the rounding of its entries; the diagonal holds half or more of each row. reset_flags[b, 0] = 1 in every stream; the runs of frames from one 1 to the next (utterances) hold 1 to 16 frames, and some hold exactly 16.
All inputs are finite; a program needn't handle non-finite values.
Results may differ from a plain program's by a relative error of at most 0.012.
Values may be sent and summed in bfloat16 or wider, within the bound.
No kernel may reach another device: no remote copies, remote signals or barrier semaphores. Data moves between devices by JAX's collectives and lax.ppermute only.
A program may use at most 64 MiB of HBM per device.

v0:
```python
import jax
import jax.numpy as jnp
from jax import lax
from jax.sharding import PartitionSpec as P

SPAN = 1
acoustic = 0.1


def in_one_piece(arrays, axis, dim, along):
    columns = [a.reshape(*a.shape[:along], -1) for a in arrays]
    both = jnp.concatenate(columns, axis=along)
    out, at, gathered = (lax.all_gather(both, axis, axis=dim, tiled=True), 0, [])
    for a, column in zip(arrays, columns):
        piece = out[..., at : at + column.shape[along]]
        gathered.append(piece.reshape(*piece.shape[:along], *a.shape[along:]))
        at += column.shape[along]
    return tuple(gathered)


def passed_along(block, axis, distance):
    devices = range(lax.axis_size(axis))
    route = [(i - distance, i) for i in devices if i - distance in devices]
    return lax.ppermute(block, axis, route)


def local_scores(features, gauss_means, precisions):
    streams, frames, feat_width = features.shape
    highest = lax.Precision.HIGHEST
    flat_feats = features.reshape(streams * frames, feat_width)
    quadratic = jnp.dot(flat_feats * flat_feats, (-0.5 * precisions).T, precision=highest)
    linear_part = jnp.dot(flat_feats, (precisions * gauss_means).T, precision=highest)
    offset = 0.5 * jnp.sum(jnp.log(precisions) - precisions * gauss_means * gauss_means, axis=1)
    return (acoustic * (quadratic + linear_part + offset)).reshape(
        streams, frames, gauss_means.shape[0]
    )


def run_block(emission_t, reset_t, trans, trans_back, prior_dist, alpha_in, beta_in):
    states = trans.shape[0]

    def forward_step(alpha_prev, inputs):
        emit_row, reset_row = inputs
        predicted = jnp.dot(
            alpha_prev.astype(jnp.bfloat16), trans, preferred_element_type=jnp.float32
        )
        predicted = jnp.where(reset_row[:, None] == 1, prior_dist[None, :], predicted)
        weighted = emit_row * predicted
        norm_total = jnp.sum(weighted, axis=1)
        alpha_next = weighted / norm_total[:, None]
        return (alpha_next, (alpha_next, jnp.log(norm_total)))

    alpha_out, (alphas, log_norms) = lax.scan(forward_step, alpha_in, (emission_t, reset_t))

    def backward_step(beta_next, inputs):
        emit_row, reset_row = inputs
        spread = jnp.dot(
            (emit_row * beta_next).astype(jnp.bfloat16),
            trans_back,
            preferred_element_type=jnp.float32,
        )
        spread = spread / jnp.sum(spread, axis=1, keepdims=True)
        beta_prev = jnp.where(reset_row[:, None] == 1, 1.0 / states, spread)
        return (beta_prev, beta_next)

    beta_out, betas = lax.scan(backward_step, beta_in, (emission_t, reset_t), reverse=True)
    return (alpha_out, alphas, log_norms, beta_out, betas)


def run_chain(scores, resets, trans, trans_back, prior_dist, relay_step, relays):
    maxima = jnp.max(scores, axis=2, keepdims=True)
    emission_t = jnp.swapaxes(jnp.exp(scores - maxima), 0, 1)
    reset_t = jnp.swapaxes(resets, 0, 1)
    streams, states = (scores.shape[0], scores.shape[2])
    alpha_in = jnp.full((streams, states), 1.0 / states, jnp.float32)
    beta_in = alpha_in
    for relay_turn in range(relays + 1):
        alpha_out, alphas, log_norms, beta_out, betas = run_block(
            emission_t, reset_t, trans, trans_back, prior_dist, alpha_in, beta_in
        )
        if relay_turn < relays:
            alpha_in, beta_in = relay_step(alpha_out, beta_out)
    product = alphas * betas
    posterior = (product / jnp.sum(product, axis=2, keepdims=True)).astype(jnp.bfloat16)
    return (jnp.swapaxes(posterior, 0, 1), jnp.swapaxes(log_norms, 0, 1))


def per_device(features, gauss_means, precisions, transitions, initial, reset_flags):
    trans, prior_raw = in_one_piece((transitions, initial), "state", 0, 1)
    trans_back = trans.T
    states = trans.shape[0]
    prior_float = prior_raw.astype(jnp.float32)
    prior_dist = prior_float / jnp.sum(prior_float)
    scores = local_scores(features, gauss_means, precisions)
    group = lax.axis_size("state")
    place = lax.axis_index("state")
    blocks = lax.axis_size("tm")
    block_place = lax.axis_index("tm")
    quarter = features.shape[1] // group
    is_last = block_place * group + place == blocks * group - 1

    def relay_step(alpha_out, beta_out):
        alpha_next = passed_along(alpha_out, ("tm", "state"), 1)
        beta_next = passed_along(beta_out, ("tm", "state"), -1)
        beta_next = jnp.where(is_last, 1.0 / states, beta_next)
        return (alpha_next, beta_next)

    my_scores = lax.all_to_all(scores, "state", split_axis=1, concat_axis=2, tiled=True)
    my_flags = lax.dynamic_slice_in_dim(reset_flags, place * quarter, quarter, 1)
    posterior, evidence = run_chain(
        my_scores, my_flags, trans, trans_back, prior_dist, relay_step, SPAN * group
    )
    posteriors = lax.all_to_all(posterior, "state", split_axis=2, concat_axis=1, tiled=True)
    return (posteriors, evidence)


def solution(mesh):
    return jax.shard_map(
        per_device,
        mesh=mesh,
        in_specs=(
            P(None, "tm", None),
            P("state", None),
            P("state", None),
            P("state", None),
            P("state"),
            P(None, "tm"),
        ),
        out_specs=(P(None, "tm", "state"), P(None, ("tm", "state"))),
        check_vma=False,
    )
```

profile of v0, /device:TPU:257, one launch (start us, length us, event | category | flops | bytes accessed | tf_op | source)
XLA Modules:
  0.0 149.7 jit_solution(1743918318548357542)
XLA Ops:
  7.2 1.5 %copy.41 = bf16[512,1024]{0,1:T(8,128)(2,1)S(1)} copy(bf16[512,1024]{1,0:T(8,128)(2,1)} %param.21) | data formatting | bytes 2097152 | tf_op args[3]
  8.8 1.1 pad_maximum_fusion
  11.0 1.1 fusion.30
  12.0 1.2 fusion.27
  13.2 0.7 copy.38
  14.0 4.0 %all-to-all-start = ((f32[4,16,512]{2,0,1:T(4,128)}), f32[4,16,512]{2,0,1:T(4,128)S(1)}, u32[]{:S(2)}, u32[]{:S(2)}) async-start(f32[4,16,512]{2,0,1:T(4,128)} %copy.38), calls=%async_computation | async-start | bytes 262144 | tf_op jit(solution)/shard_map/all_to_all | solution.py:108
  18.2 0.9 all-to-all-done
  19.4 11.7 %all-gather.2.cloned.1.call-done = bf16[1024,1025]{0,1:T(8,128)(2,1)} async-done(((bf16[512,1025]{0,1:T(8,128)(2,1)}), bf16[1024,1025]{0,1:T(8,128)(2,1)}) %all-gather.2.cloned.1.call-update) | async-done | bytes 2099216 | tf_op jit(solution)/shard_map/all_gather | solution.py:13
  31.1 3.5 %slice_bitcast_fusion = (bf16[1024,1024]{1,0:T(8,128)(2,1)S(1)}, bf16[1024,1024]{0,1:T(8,128)(2,1)}) fusion(bf16[1024,1025]{0,1:T(8,128)(2,1)} %all-gather.2.cloned.1.call-done), kind=kLoop, calls=%fused_computation.68 | loop fusion | bytes 6291456 | tf_op jit(solution)/shard_map/transpose | solution.py:90
  34.6 3.9 %copy.42 = bf16[1024,1024]{1,0:T(8,128)(2,1)} copy(bf16[1024,1024]{0,1:T(8,128)(2,1)} %get-tuple-element.648) | data formatting | bytes 4194304
  38.5 1.4 fusion.37
  39.9 1.3 fusion.36
  41.2 17.6 %while.84 = (s32[]{:T(128)}, f32[4,1024]{1,0:T(4,128)S(1)}, f32[8,4,1024]{2,1,0:T(4,128)S(1)}, s32[8,4]{1,0:T(8,128)S(1)}, f32[1024]{0:T(1024)S(1)}, /*index=5*/bf16[1024,1024]{1,0:T(8,128)(2,1)}, s32[]{:T(128)}, s32[]{:T(128)}) while((s32[]{:T(128)}, f32[4,1024]{1,0:T(4,128)S(1)}, f32[8,4,1024]{2,1,0:T(4,128)S(1)}, ...), condition=%wide.region_5.6_spmd.clone, body=%wide.region_3.5_spmd.clone.sunk | while | flops 8409091 | bytes 2183327 | solution.py:53
  41.2 2.1 %fusion.76 = (f32[4]{0:T(128)S(1)}, f32[4,1024]{1,0:T(4,128)S(1)}) fusion(bf16[1024,1024]{1,0:T(8,128)(2,1)} %get-tuple-element.916, f32[4,1024]{1,0:T(4,128)S(1)} %get-tuple-element.904, pred[]{:T(512)S(6)} %compare.6, f32[1024]{0:T(1024)S(1)} %get-tuple-element.915, pred[4]{0:T(512)(128)(4,1)S(1)} %compare_bitcast_fusion.16, ...), kind=kOutput, calls=%fused_computation.73.clone.1 | convolution fusion | flops 8404988 | bytes 2150425 | tf_op jit(solution)/shard_map/while/body/eval_jaxpr/dot_general | solution.py:44
  43.4 2.1 %fusion.76 = (f32[4]{0:T(128)S(1)}, f32[4,1024]{1,0:T(4,128)S(1)}) fusion(bf16[1024,1024]{1,0:T(8,128)(2,1)} %get-tuple-element.916, f32[4,1024]{1,0:T(4,128)S(1)} %get-tuple-element.904, pred[]{:T(512)S(6)} %compare.6, f32[1024]{0:T(1024)S(1)} %get-tuple-element.915, pred[4]{0:T(512)(128)(4,1)S(1)} %compare_bitcast_fusion.16, ...), kind=kOutput, calls=%fused_computation.73.clone.1 | convolution fusion | flops 8404988 | bytes 2150425 | tf_op jit(solution)/shard_map/while/body/eval_jaxpr/dot_general | solution.py:44
  45.6 2.1 %fusion.76 = (f32[4]{0:T(128)S(1)}, f32[4,1024]{1,0:T(4,128)S(1)}) fusion(bf16[1024,1024]{1,0:T(8,128)(2,1)} %get-tuple-element.916, f32[4,1024]{1,0:T(4,128)S(1)} %get-tuple-element.904, pred[]{:T(512)S(6)} %compare.6, f32[1024]{0:T(1024)S(1)} %get-tuple-element.915, pred[4]{0:T(512)(128)(4,1)S(1)} %compare_bitcast_fusion.16, ...), kind=kOutput, calls=%fused_computation.73.clone.1 | convolution fusion | flops 8404988 | bytes 2150425 | tf_op jit(solution)/shard_map/while/body/eval_jaxpr/dot_general | solution.py:44
  47.8 2.1 %fusion.76 = (f32[4]{0:T(128)S(1)}, f32[4,1024]{1,0:T(4,128)S(1)}) fusion(bf16[1024,1024]{1,0:T(8,128)(2,1)} %get-tuple-element.916, f32[4,1024]{1,0:T(4,128)S(1)} %get-tuple-element.904, pred[]{:T(512)S(6)} %compare.6, f32[1024]{0:T(1024)S(1)} %get-tuple-element.915, pred[4]{0:T(512)(128)(4,1)S(1)} %compare_bitcast_fusion.16, ...), kind=kOutput, calls=%fused_computation.73.clone.1 | convolution fusion | flops 8404988 | bytes 2150425 | tf_op jit(solution)/shard_map/while/body/eval_jaxpr/dot_general | solution.py:44
  50.0 2.1 %fusion.76 = (f32[4]{0:T(128)S(1)}, f32[4,1024]{1,0:T(4,128)S(1)}) fusion(bf16[1024,1024]{1,0:T(8,128)(2,1)} %get-tuple-element.916, f32[4,1024]{1,0:T(4,128)S(1)} %get-tuple-element.904, pred[]{:T(512)S(6)} %compare.6, f32[1024]{0:T(1024)S(1)} %get-tuple-element.915, pred[4]{0:T(512)(128)(4,1)S(1)} %compare_bitcast_fusion.16, ...), kind=kOutput, calls=%fused_computation.73.clone.1 | convolution fusion | flops 8404988 | bytes 2150425 | tf_op jit(solution)/shard_map/while/body/eval_jaxpr/dot_general | solution.py:44
  52.2 2.1 %fusion.76 = (f32[4]{0:T(128)S(1)}, f32[4,1024]{1,0:T(4,128)S(1)}) fusion(bf16[1024,1024]{1,0:T(8,128)(2,1)} %get-tuple-element.916, f32[4,1024]{1,0:T(4,128)S(1)} %get-tuple-element.904, pred[]{:T(512)S(6)} %compare.6, f32[1024]{0:T(1024)S(1)} %get-tuple-element.915, pred[4]{0:T(512)(128)(4,1)S(1)} %compare_bitcast_fusion.16, ...), kind=kOutput, calls=%fused_computation.73.clone.1 | convolution fusion | flops 8404988 | bytes 2150425 | tf_op jit(solution)/shard_map/while/body/eval_jaxpr/dot_general | solution.py:44
  54.4 2.1 %fusion.76 = (f32[4]{0:T(128)S(1)}, f32[4,1024]{1,0:T(4,128)S(1)}) fusion(bf16[1024,1024]{1,0:T(8,128)(2,1)} %get-tuple-element.916, f32[4,1024]{1,0:T(4,128)S(1)} %get-tuple-element.904, pred[]{:T(512)S(6)} %compare.6, f32[1024]{0:T(1024)S(1)} %get-tuple-element.915, pred[4]{0:T(512)(128)(4,1)S(1)} %compare_bitcast_fusion.16, ...), kind=kOutput, calls=%fused_computation.73.clone.1 | convolution fusion | flops 8404988 | bytes 2150425 | tf_op jit(solution)/shard_map/while/body/eval_jaxpr/dot_general | solution.py:44
  56.6 2.1 %fusion.76 = (f32[4]{0:T(128)S(1)}, f32[4,1024]{1,0:T(4,128)S(1)}) fusion(bf16[1024,1024]{1,0:T(8,128)(2,1)} %get-tuple-element.916, f32[4,1024]{1,0:T(4,128)S(1)} %get-tuple-element.904, pred[]{:T(512)S(6)} %compare.6, f32[1024]{0:T(1024)S(1)} %get-tuple-element.915, pred[4]{0:T(512)(128)(4,1)S(1)} %compare_bitcast_fusion.16, ...), kind=kOutput, calls=%fused_computation.73.clone.1 | convolution fusion | flops 8404988 | bytes 2150425 | tf_op jit(solution)/shard_map/while/body/eval_jaxpr/dot_general | solution.py:44
  58.8 3.2 %collective-permute-start = (f32[4,1024]{1,0:T(4,128)S(1)}, f32[4,1024]{1,0:T(4,128)S(1)}, u32[]{:S(2)}, u32[]{:S(2)}) collective-permute-start(f32[4,1024]{1,0:T(4,128)S(1)} %get-tuple-element.437), channel_id=1, source_target_pairs={{0,1},{1,2},{2,3},{3,4},{4,5},{5,6},{6,7},{7,8},{8,9},{9,10},{10,1... | collective-permute-start | bytes 49160 | tf_op jit(solution)/shard_map/ppermute | solution.py:24
  62.0 4.8 %while.85 = (s32[]{:T(128)}, f32[4,1024]{1,0:T(4,128)S(1)}, s32[8,4]{1,0:T(8,128)S(1)}, f32[8,4,1024]{2,1,0:T(4,128)S(1)}, bf16[1024,1024]{1,0:T(8,128)(2,1)S(1)}, /*index=5*/s32[]{:T(128)}, s32[]{:T(128)}, s32[]{:T(128)}) while((s32[]{:T(128)}, f32[4,1024]{1,0:T(4,128)S(1)}, s32[8,4]{1,0:T(8,128)S(1)}, ...), condition=%wide.region_14.15_spmd.clone, body=%wide.region_12.14_spmd.clone.sunk | while | flops 8413188 | bytes 2179243 | solution.py:66
  63.2 0.5 fusion.78
  65.0 0.5 fusion.78
  66.2 0.5 fusion.78
  66.8 1.9 %collective-permute-start.2 = (f32[4,1024]{1,0:T(4,128)S(1)}, f32[4,1024]{1,0:T(4,128)S(1)}, u32[]{:S(2)}, u32[]{:S(2)}) collective-permute-start(f32[4,1024]{1,0:T(4,128)S(1)} %get-tuple-element.440), channel_id=1, source_target_pairs={{1,0},{2,1},{3,2},{4,3},{5,4},{6,5},{7,6},{8,7},{9,8},{10,9},{11,1... | collective-permute-start | bytes 49160 | tf_op jit(solution)/shard_map/ppermute | solution.py:24
  68.7 17.6 %while.80 = (s32[]{:T(128)}, f32[4,1024]{1,0:T(4,128)S(1)}, f32[8,4,1024]{2,1,0:T(4,128)S(1)}, s32[8,4]{1,0:T(8,128)S(1)}, f32[1024]{0:T(1024)S(1)}, /*index=5*/bf16[1024,1024]{1,0:T(8,128)(2,1)}, s32[]{:T(128)}) while((s32[]{:T(128)}, f32[4,1024]{1,0:T(4,128)S(1)}, f32[8,4,1024]{2,1,0:T(4,128)S(1)}, s32[8,4]{1,0:T(8,128)S(1)}, ...), condition=%wide.region_8.9_spmd, body=%wide.region_6.8_spmd.sunk | while | flops 8409090 | bytes 2183309 | solution.py:53
  68.7 2.1 %fusion.67 = (f32[4]{0:T(128)S(1)}, f32[4,1024]{1,0:T(4,128)S(1)}) fusion(bf16[1024,1024]{1,0:T(8,128)(2,1)} %get-tuple-element.938, f32[4,1024]{1,0:T(4,128)S(1)} %get-tuple-element.927, f32[1024]{0:T(1024)S(1)} %get-tuple-element.937, pred[4]{0:T(512)(128)(4,1)S(1)} %compare_bitcast_fusion.12, f32[8,4,1024]{2,1,0:T(4,128)S(1)} %get-tuple-element.935, ...), kind=kOutput, calls=%fused_computation.69.clone.1 | convolution fusion | flops 8404988 | bytes 2150424 | tf_op jit(solution)/shard_map/while/body/eval_jaxpr/dot_general | solution.py:44
  70.9 2.1 %fusion.67 = (f32[4]{0:T(128)S(1)}, f32[4,1024]{1,0:T(4,128)S(1)}) fusion(bf16[1024,1024]{1,0:T(8,128)(2,1)} %get-tuple-element.938, f32[4,1024]{1,0:T(4,128)S(1)} %get-tuple-element.927, f32[1024]{0:T(1024)S(1)} %get-tuple-element.937, pred[4]{0:T(512)(128)(4,1)S(1)} %compare_bitcast_fusion.12, f32[8,4,1024]{2,1,0:T(4,128)S(1)} %get-tuple-element.935, ...), kind=kOutput, calls=%fused_computation.69.clone.1 | convolution fusion | flops 8404988 | bytes 2150424 | tf_op jit(solution)/shard_map/while/body/eval_jaxpr/dot_general | solution.py:44
  73.1 2.1 %fusion.67 = (f32[4]{0:T(128)S(1)}, f32[4,1024]{1,0:T(4,128)S(1)}) fusion(bf16[1024,1024]{1,0:T(8,128)(2,1)} %get-tuple-element.938, f32[4,1024]{1,0:T(4,128)S(1)} %get-tuple-element.927, f32[1024]{0:T(1024)S(1)} %get-tuple-element.937, pred[4]{0:T(512)(128)(4,1)S(1)} %compare_bitcast_fusion.12, f32[8,4,1024]{2,1,0:T(4,128)S(1)} %get-tuple-element.935, ...), kind=kOutput, calls=%fused_computation.69.clone.1 | convolution fusion | flops 8404988 | bytes 2150424 | tf_op jit(solution)/shard_map/while/body/eval_jaxpr/dot_general | solution.py:44
  75.3 2.1 %fusion.67 = (f32[4]{0:T(128)S(1)}, f32[4,1024]{1,0:T(4,128)S(1)}) fusion(bf16[1024,1024]{1,0:T(8,128)(2,1)} %get-tuple-element.938, f32[4,1024]{1,0:T(4,128)S(1)} %get-tuple-element.927, f32[1024]{0:T(1024)S(1)} %get-tuple-element.937, pred[4]{0:T(512)(128)(4,1)S(1)} %compare_bitcast_fusion.12, f32[8,4,1024]{2,1,0:T(4,128)S(1)} %get-tuple-element.935, ...), kind=kOutput, calls=%fused_computation.69.clone.1 | convolution fusion | flops 8404988 | bytes 2150424 | tf_op jit(solution)/shard_map/while/body/eval_jaxpr/dot_general | solution.py:44
  77.5 2.1 %fusion.67 = (f32[4]{0:T(128)S(1)}, f32[4,1024]{1,0:T(4,128)S(1)}) fusion(bf16[1024,1024]{1,0:T(8,128)(2,1)} %get-tuple-element.938, f32[4,1024]{1,0:T(4,128)S(1)} %get-tuple-element.927, f32[1024]{0:T(1024)S(1)} %get-tuple-element.937, pred[4]{0:T(512)(128)(4,1)S(1)} %compare_bitcast_fusion.12, f32[8,4,1024]{2,1,0:T(4,128)S(1)} %get-tuple-element.935, ...), kind=kOutput, calls=%fused_computation.69.clone.1 | convolution fusion | flops 8404988 | bytes 2150424 | tf_op jit(solution)/shard_map/while/body/eval_jaxpr/dot_general | solution.py:44
  79.7 2.1 %fusion.67 = (f32[4]{0:T(128)S(1)}, f32[4,1024]{1,0:T(4,128)S(1)}) fusion(bf16[1024,1024]{1,0:T(8,128)(2,1)} %get-tuple-element.938, f32[4,1024]{1,0:T(4,128)S(1)} %get-tuple-element.927, f32[1024]{0:T(1024)S(1)} %get-tuple-element.937, pred[4]{0:T(512)(128)(4,1)S(1)} %compare_bitcast_fusion.12, f32[8,4,1024]{2,1,0:T(4,128)S(1)} %get-tuple-element.935, ...), kind=kOutput, calls=%fused_computation.69.clone.1 | convolution fusion | flops 8404988 | bytes 2150424 | tf_op jit(solution)/shard_map/while/body/eval_jaxpr/dot_general | solution.py:44
  81.9 2.1 %fusion.67 = (f32[4]{0:T(128)S(1)}, f32[4,1024]{1,0:T(4,128)S(1)}) fusion(bf16[1024,1024]{1,0:T(8,128)(2,1)} %get-tuple-element.938, f32[4,1024]{1,0:T(4,128)S(1)} %get-tuple-element.927, f32[1024]{0:T(1024)S(1)} %get-tuple-element.937, pred[4]{0:T(512)(128)(4,1)S(1)} %compare_bitcast_fusion.12, f32[8,4,1024]{2,1,0:T(4,128)S(1)} %get-tuple-element.935, ...), kind=kOutput, calls=%fused_computation.69.clone.1 | convolution fusion | flops 8404988 | bytes 2150424 | tf_op jit(solution)/shard_map/while/body/eval_jaxpr/dot_general | solution.py:44
  84.1 2.1 %fusion.67 = (f32[4]{0:T(128)S(1)}, f32[4,1024]{1,0:T(4,128)S(1)}) fusion(bf16[1024,1024]{1,0:T(8,128)(2,1)} %get-tuple-element.938, f32[4,1024]{1,0:T(4,128)S(1)} %get-tuple-element.927, f32[1024]{0:T(1024)S(1)} %get-tuple-element.937, pred[4]{0:T(512)(128)(4,1)S(1)} %compare_bitcast_fusion.12, f32[8,4,1024]{2,1,0:T(4,128)S(1)} %get-tuple-element.935, ...), kind=kOutput, calls=%fused_computation.69.clone.1 | convolution fusion | flops 8404988 | bytes 2150424 | tf_op jit(solution)/shard_map/while/body/eval_jaxpr/dot_general | solution.py:44
  86.3 3.6 %collective-permute-start.1 = (f32[4,1024]{1,0:T(4,128)S(1)}, f32[4,1024]{1,0:T(4,128)S(1)}, u32[]{:S(2)}, u32[]{:S(2)}) collective-permute-start(f32[4,1024]{1,0:T(4,128)S(1)} %get-tuple-element.438), channel_id=1, source_target_pairs={{0,1},{1,2},{2,3},{3,4},{4,5},{5,6},{6,7},{7,8},{8,9},{9,10},{10,1... | collective-permute-start | bytes 49160 | tf_op jit(solution)/shard_map/ppermute | solution.py:24
  90.0 4.8 %while.82 = (s32[]{:T(128)}, f32[4,1024]{1,0:T(4,128)S(1)}, s32[8,4]{1,0:T(8,128)S(1)}, f32[8,4,1024]{2,1,0:T(4,128)S(1)}, bf16[1024,1024]{1,0:T(8,128)(2,1)S(1)}, /*index=5*/s32[]{:T(128)}, s32[]{:T(128)}) while((s32[]{:T(128)}, f32[4,1024]{1,0:T(4,128)S(1)}, s32[8,4]{1,0:T(8,128)S(1)}, f32[8,4,1024]{2,1,0:T(4,128)S(1)}, ...), condition=%wide.region_17.18_spmd, body=%wide.region_15.17_spmd.sunk | while | flops 8409091 | bytes 2179225 | solution.py:66
  90.0 0.5 fusion.72
  90.6 0.5 fusion.72
  91.2 0.5 fusion.72
  91.7 0.5 fusion.72
  92.3 0.5 fusion.72
  92.9 0.5 fusion.72
  93.5 0.5 fusion.72
  94.1 0.5 fusion.72
  94.7 6.3 %collective-permute-start.3 = (f32[4,1024]{1,0:T(4,128)S(1)}, f32[4,1024]{1,0:T(4,128)S(1)}, u32[]{:S(2)}, u32[]{:S(2)}) collective-permute-start(f32[4,1024]{1,0:T(4,128)S(1)} %get-tuple-element.441), channel_id=1, source_target_pairs={{1,0},{2,1},{3,2},{4,3},{5,4},{6,5},{7,6},{8,7},{9,8},{10,9},{11,1... | collective-permute-start | bytes 49160 | tf_op jit(solution)/shard_map/ppermute | solution.py:24
  101.0 20.0 %while.81 = (s32[]{:T(128)}, f32[4,1024]{1,0:T(4,128)S(1)}, f32[8,4,1024]{2,0,1:T(8,128)S(1)}, f32[8,4]{1,0:T(8,128)S(1)}, f32[8,4,1024]{2,1,0:T(4,128)S(1)}, /*...) while((s32[]{:T(128)}, f32[4,1024]{1,0:T(4,128)S(1)}, ...), condition=%wide.region_11.12_spmd, body=%wide.region_9.11_spmd.sunk | while | flops 8413186 | bytes 2281725 | solution.py:53
  101.1 2.1 %fusion.69 = (f32[4]{0:T(128)S(1)}, f32[4,1024]{1,0:T(4,128)S(1)}) fusion(bf16[1024,1024]{1,0:T(8,128)(2,1)} %get-tuple-element.967, f32[4,1024]{1,0:T(4,128)S(1)} %get-tuple-element.951, f32[1024]{0:T(1024)S(1)} %get-tuple-element.966, pred[4]{0:T(512)(128)(4,1)S(1)} %compare_bitcast_fusion.13, f32[8,4,1024]{2,1,0:T(4,128)S(1)} %get-tuple-element.964, ...), kind=kOutput, calls=%fused_computation.70.clone.1 | convolution fusion | flops 8404988 | bytes 2150424 | tf_op jit(solution)/shard_map/while/body/eval_jaxpr/dot_general | solution.py:44
  103.6 2.1 %fusion.69 = (f32[4]{0:T(128)S(1)}, f32[4,1024]{1,0:T(4,128)S(1)}) fusion(bf16[1024,1024]{1,0:T(8,128)(2,1)} %get-tuple-element.967, f32[4,1024]{1,0:T(4,128)S(1)} %get-tuple-element.951, f32[1024]{0:T(1024)S(1)} %get-tuple-element.966, pred[4]{0:T(512)(128)(4,1)S(1)} %compare_bitcast_fusion.13, f32[8,4,1024]{2,1,0:T(4,128)S(1)} %get-tuple-element.964, ...), kind=kOutput, calls=%fused_computation.70.clone.1 | convolution fusion | flops 8404988 | bytes 2150424 | tf_op jit(solution)/shard_map/while/body/eval_jaxpr/dot_general | solution.py:44
  106.1 2.1 %fusion.69 = (f32[4]{0:T(128)S(1)}, f32[4,1024]{1,0:T(4,128)S(1)}) fusion(bf16[1024,1024]{1,0:T(8,128)(2,1)} %get-tuple-element.967, f32[4,1024]{1,0:T(4,128)S(1)} %get-tuple-element.951, f32[1024]{0:T(1024)S(1)} %get-tuple-element.966, pred[4]{0:T(512)(128)(4,1)S(1)} %compare_bitcast_fusion.13, f32[8,4,1024]{2,1,0:T(4,128)S(1)} %get-tuple-element.964, ...), kind=kOutput, calls=%fused_computation.70.clone.1 | convolution fusion | flops 8404988 | bytes 2150424 | tf_op jit(solution)/shard_map/while/body/eval_jaxpr/dot_general | solution.py:44
  108.6 2.1 %fusion.69 = (f32[4]{0:T(128)S(1)}, f32[4,1024]{1,0:T(4,128)S(1)}) fusion(bf16[1024,1024]{1,0:T(8,128)(2,1)} %get-tuple-element.967, f32[4,1024]{1,0:T(4,128)S(1)} %get-tuple-element.951, f32[1024]{0:T(1024)S(1)} %get-tuple-element.966, pred[4]{0:T(512)(128)(4,1)S(1)} %compare_bitcast_fusion.13, f32[8,4,1024]{2,1,0:T(4,128)S(1)} %get-tuple-element.964, ...), kind=kOutput, calls=%fused_computation.70.clone.1 | convolution fusion | flops 8404988 | bytes 2150424 | tf_op jit(solution)/shard_map/while/body/eval_jaxpr/dot_general | solution.py:44
  111.1 2.1 %fusion.69 = (f32[4]{0:T(128)S(1)}, f32[4,1024]{1,0:T(4,128)S(1)}) fusion(bf16[1024,1024]{1,0:T(8,128)(2,1)} %get-tuple-element.967, f32[4,1024]{1,0:T(4,128)S(1)} %get-tuple-element.951, f32[1024]{0:T(1024)S(1)} %get-tuple-element.966, pred[4]{0:T(512)(128)(4,1)S(1)} %compare_bitcast_fusion.13, f32[8,4,1024]{2,1,0:T(4,128)S(1)} %get-tuple-element.964, ...), kind=kOutput, calls=%fused_computation.70.clone.1 | convolution fusion | flops 8404988 | bytes 2150424 | tf_op jit(solution)/shard_map/while/body/eval_jaxpr/dot_general | solution.py:44
  113.6 2.1 %fusion.69 = (f32[4]{0:T(128)S(1)}, f32[4,1024]{1,0:T(4,128)S(1)}) fusion(bf16[1024,1024]{1,0:T(8,128)(2,1)} %get-tuple-element.967, f32[4,1024]{1,0:T(4,128)S(1)} %get-tuple-element.951, f32[1024]{0:T(1024)S(1)} %get-tuple-element.966, pred[4]{0:T(512)(128)(4,1)S(1)} %compare_bitcast_fusion.13, f32[8,4,1024]{2,1,0:T(4,128)S(1)} %get-tuple-element.964, ...), kind=kOutput, calls=%fused_computation.70.clone.1 | convolution fusion | flops 8404988 | bytes 2150424 | tf_op jit(solution)/shard_map/while/body/eval_jaxpr/dot_general | solution.py:44
  116.0 2.1 %fusion.69 = (f32[4]{0:T(128)S(1)}, f32[4,1024]{1,0:T(4,128)S(1)}) fusion(bf16[1024,1024]{1,0:T(8,128)(2,1)} %get-tuple-element.967, f32[4,1024]{1,0:T(4,128)S(1)} %get-tuple-element.951, f32[1024]{0:T(1024)S(1)} %get-tuple-element.966, pred[4]{0:T(512)(128)(4,1)S(1)} %compare_bitcast_fusion.13, f32[8,4,1024]{2,1,0:T(4,128)S(1)} %get-tuple-element.964, ...), kind=kOutput, calls=%fused_computation.70.clone.1 | convolution fusion | flops 8404988 | bytes 2150424 | tf_op jit(solution)/shard_map/while/body/eval_jaxpr/dot_general | solution.py:44
  118.5 2.1 %fusion.69 = (f32[4]{0:T(128)S(1)}, f32[4,1024]{1,0:T(4,128)S(1)}) fusion(bf16[1024,1024]{1,0:T(8,128)(2,1)} %get-tuple-element.967, f32[4,1024]{1,0:T(4,128)S(1)} %get-tuple-element.951, f32[1024]{0:T(1024)S(1)} %get-tuple-element.966, pred[4]{0:T(512)(128)(4,1)S(1)} %compare_bitcast_fusion.13, f32[8,4,1024]{2,1,0:T(4,128)S(1)} %get-tuple-element.964, ...), kind=kOutput, calls=%fused_computation.70.clone.1 | convolution fusion | flops 8404988 | bytes 2150424 | tf_op jit(solution)/shard_map/while/body/eval_jaxpr/dot_general | solution.py:44
  121.1 6.2 %while.83 = (s32[]{:T(128)}, f32[4,1024]{1,0:T(4,128)S(1)}, f32[8,4,1024]{2,0,1:T(8,128)S(1)}, s32[8,4]{1,0:T(8,128)S(1)}, f32[8,4,1024]{2,1,0:T(4,128)S(1)}, /*...) while((s32[]{:T(128)}, f32[4,1024]{1,0:T(4,128)S(1)}, ...), condition=%wide.region_20.21_spmd, body=%wide.region_18.20_spmd.sunk | while | flops 8409091 | bytes 2244781 | solution.py:66
  121.1 0.5 fusion.74
  127.4 0.7 copy.47
  128.1 1.1 reshape.120
  129.2 10.6 %all_to_all.36 = bf16[2,2,8192]{2,1,0:T(2,128)(2,1)S(1)} all-to-all(bf16[2,2,8192]{2,1,0:T(2,128)(2,1)S(1)} %reshape.120), channel_id=1, replica_groups=mesh['tm'=256,'state'=2] {'state'}, dimensions={0} | all-to-all | bytes 131072 | tf_op jit(solution)/shard_map/all_to_all | solution.py:113
  139.8 1.2 reshape.121
  141.0 1.2 copy.48
  142.2 0.7 copy.49
  (196 shorter events, 15.4 us)
Async XLA Ops:
  7.2 10.8 %copy-start = (s32[4,16]{1,0:T(4,128)S(1)}, s32[4,16]{1,0:T(4,128)}, u32[]{:S(2)}) copy-start(s32[4,16]{1,0:T(4,128)} %param.23) | copy-start | bytes 772
  7.2 1.6 %copy-start.4 = (bf16[512]{0:T(512)(128)(2,1)S(1)}, bf16[512]{0:T(512)(128)(2,1)}, u32[]{:S(2)}) copy-start(bf16[512]{0:T(512)(128)(2,1)} %param.22) | copy-start | bytes 3076
  7.2 23.9 %all-gather.2.cloned.1.call-start = ((), (), s32[]{:S(2)}) async-start(), calls=%async_computation.2 | async-start | bytes 3170304 | tf_op jit(solution)/shard_map/all_gather | solution.py:13
  8.8 1.6 %copy-start.1 = (f32[512,512]{1,0:T(8,128)S(1)}, f32[512,512]{1,0:T(8,128)}, u32[]{:S(2)}) copy-start(f32[512,512]{1,0:T(8,128)} %param.20) | copy-start | bytes 3145732
  8.8 1.9 %copy-start.2 = (f32[512,512]{1,0:T(8,128)S(1)}, f32[512,512]{1,0:T(8,128)}, u32[]{:S(2)}) copy-start(f32[512,512]{1,0:T(8,128)} %param.19) | copy-start | bytes 3145732
  9.9 1.1 copy-start.3
  14.0 5.2 %all-to-all-start = ((f32[4,16,512]{2,0,1:T(4,128)}), f32[4,16,512]{2,0,1:T(4,128)S(1)}, u32[]{:S(2)}, u32[]{:S(2)}) async-start(f32[4,16,512]{2,0,1:T(4,128)} %copy.38), calls=%async_computation | async-start | bytes 262144 | tf_op jit(solution)/shard_map/all_to_all | solution.py:108
  58.8 9.9 %collective-permute-start = (f32[4,1024]{1,0:T(4,128)S(1)}, f32[4,1024]{1,0:T(4,128)S(1)}, u32[]{:S(2)}, u32[]{:S(2)}) collective-permute-start(f32[4,1024]{1,0:T(4,128)S(1)} %get-tuple-element.437), channel_id=1, source_target_pairs={{0,1},{1,2},{2,3},{3,4},{4,5},{5,6},{6,7},{7,8},{8,9},{9,10},{10,1... | collective-permute-start | bytes 49160 | tf_op jit(solution)/shard_map/ppermute | solution.py:24
  66.8 23.2 %collective-permute-start.2 = (f32[4,1024]{1,0:T(4,128)S(1)}, f32[4,1024]{1,0:T(4,128)S(1)}, u32[]{:S(2)}, u32[]{:S(2)}) collective-permute-start(f32[4,1024]{1,0:T(4,128)S(1)} %get-tuple-element.440), channel_id=1, source_target_pairs={{1,0},{2,1},{3,2},{4,3},{5,4},{6,5},{7,6},{8,7},{9,8},{10,9},{11,1... | collective-permute-start | bytes 49160 | tf_op jit(solution)/shard_map/ppermute | solution.py:24
  86.3 14.7 %collective-permute-start.1 = (f32[4,1024]{1,0:T(4,128)S(1)}, f32[4,1024]{1,0:T(4,128)S(1)}, u32[]{:S(2)}, u32[]{:S(2)}) collective-permute-start(f32[4,1024]{1,0:T(4,128)S(1)} %get-tuple-element.438), channel_id=1, source_target_pairs={{0,1},{1,2},{2,3},{3,4},{4,5},{5,6},{6,7},{7,8},{8,9},{9,10},{10,1... | collective-permute-start | bytes 49160 | tf_op jit(solution)/shard_map/ppermute | solution.py:24
  94.7 26.3 %collective-permute-start.3 = (f32[4,1024]{1,0:T(4,128)S(1)}, f32[4,1024]{1,0:T(4,128)S(1)}, u32[]{:S(2)}, u32[]{:S(2)}) collective-permute-start(f32[4,1024]{1,0:T(4,128)S(1)} %get-tuple-element.441), channel_id=1, source_target_pairs={{1,0},{2,1},{3,2},{4,3},{5,4},{6,5},{7,6},{8,7},{9,8},{10,9},{11,1... | collective-permute-start | bytes 49160 | tf_op jit(solution)/shard_map/ppermute | solution.py:24
Sparse Core Ops, SparseCore 0:
  10.1 20.9 all-gather.1
where the time goes:
time: 151 us; the launch traced here: 150 us
  matrix products  64.5 us (43%)
  starting transfers between devices  19.1 us (13%)
  local copies, waits for them, and re-layouts  18.4 us (12%)
  between operations  14.3 us (9%)
  waiting for transfers between devices  12.7 us (8%)
  blocking collectives  10.6 us (7%)
  other arithmetic  9.28 us (6%)
    dot_general x24, matrix products, forward_step(): jnp.dot(alpha_prev.astype(jnp.bfloat16), trans, preferred_element_type=jn...  50.3 us
    ppermute x4, starting transfers between devices, passed_along(): return lax.ppermute(block, axis, route)  15 us
    dot_general x24, matrix products, backward_step(): jnp.dot((emit_row * beta_next).astype(jnp.bfloat16), trans_back, preferre...  11.9 us
    all_gather x1, waiting for transfers between devices, in_one_piece(): lax.all_gather(both, axis, axis=dim, tiled=True)  11.7 us
    all_to_all x1, blocking collectives, per_device(): lax.all_to_all(posterior, 'state', split_axis=2, concat_axis=1, tiled=True)  10.6 us
    unnamed x15, local copies, waits for them, and re-layouts  8.69 us
    all_to_all x1, starting transfers between devices, per_device(): lax.all_to_all(scores, 'state', split_axis=1, concat_axis=2, tiled=True)  4.04 us
    transpose x1, local copies, waits for them, and re-layouts, per_device(): trans_back = trans.T  3.51 us
  transfers between devices with their start and end apart: 6, of which 2 were waited for; matrix products, arithmetic and copies ran while one was open for 34% of the time, Pallas kernels for 0%

commit v1 on v0

--- a/solution.py
+++ b/solution.py
@@ -5,6 +5,12 @@
 
 SPAN = 1
 acoustic = 0.1
+
+
+def stacked_exchange(block, name, split, join):
+    pieces = jnp.split(block, lax.axis_size(name), axis=split)
+    received = lax.all_to_all(jnp.stack(pieces), name, 0, 0)
+    return jnp.concatenate(received, axis=join)
 
 
 def in_one_piece(arrays, axis, dim, along):
@@ -110,7 +116,7 @@
     posterior, evidence = run_chain(
         my_scores, my_flags, trans, trans_back, prior_dist, relay_step, SPAN * group
     )
-    posteriors = lax.all_to_all(posterior, "state", split_axis=2, concat_axis=1, tiled=True)
+    posteriors = stacked_exchange(posterior, "state", 2, 1)
     return (posteriors, evidence)
 
 

time: 151 us -> 144 us (0.954)
  local copies, waits for them, and re-layouts: 18.4 us -> 12.5 us
    dynamic_update_slice x40 -> x16, local copies, waits for them, and re-layouts: 2.8 us -> 0.4 us  [run_block(): lax.scan(forward_step, alpha_in, (emission_t, reset_t))]
    unnamed x15 -> x13, local copies, waits for them, and re-layouts: 8.69 us -> 6.35 us
where the time goes in v1:
time: 144 us; the launch traced here: 143 us
  matrix products  64.4 us (45%)
  starting transfers between devices  19.1 us (13%)
  between operations  14.2 us (10%)
  waiting for transfers between devices  12.7 us (9%)
  local copies, waits for them, and re-layouts  12.5 us (9%)
  blocking collectives  10.6 us (7%)
  other arithmetic  8.84 us (6%)
    dot_general x24, matrix products, forward_step(): jnp.dot(alpha_prev.astype(jnp.bfloat16), trans, preferred_element_type=jn...  50.3 us
    ppermute x4, starting transfers between devices, passed_along(): return lax.ppermute(block, axis, route)  15 us
    dot_general x24, matrix products, backward_step(): jnp.dot((emit_row * beta_next).astype(jnp.bfloat16), trans_back, preferre...  11.9 us
    all_gather x1, waiting for transfers between devices, in_one_piece(): lax.all_gather(both, axis, axis=dim, tiled=True)  11.7 us
    all_to_all x1, blocking collectives, stacked_exchange(): received = lax.all_to_all(jnp.stack(pieces), name, 0, 0)  10.6 us
    unnamed x13, local copies, waits for them, and re-layouts  6.35 us
    all_to_all x1, starting transfers between devices, per_device(): lax.all_to_all(scores, 'state', split_axis=1, concat_axis=2, tiled=True)  4.04 us
    transpose x1, local copies, waits for them, and re-layouts, per_device(): trans_back = trans.T  3.45 us
  transfers between devices with their start and end apart: 6, of which 2 were waited for; matrix products, arithmetic and copies ran while one was open for 34% of the time, Pallas kernels for 0%

profile of v1, /device:TPU:257, one launch (start us, length us, event | category | flops | bytes accessed | tf_op | source)
XLA Modules:
  0.0 143.0 jit_solution(8086318603902848213)
XLA Ops:
  7.2 1.5 %copy.19 = bf16[512,1024]{0,1:T(8,128)(2,1)S(1)} copy(bf16[512,1024]{1,0:T(8,128)(2,1)} %param.21) | data formatting | bytes 2097152 | tf_op args[3]
  8.8 1.1 pad_maximum_fusion
  11.0 1.1 fusion.30
  12.0 1.2 fusion.27
  13.2 0.7 copy.16
  14.0 4.0 %all-to-all-start = ((f32[4,16,512]{2,0,1:T(4,128)}), f32[4,16,512]{2,0,1:T(4,128)S(1)}, u32[]{:S(2)}, u32[]{:S(2)}) async-start(f32[4,16,512]{2,0,1:T(4,128)} %copy.16), calls=%async_computation | async-start | bytes 262144 | tf_op jit(solution)/shard_map/all_to_all | solution.py:114
  18.2 0.9 all-to-all-done
  19.4 11.7 %all-gather.2.cloned.1.call-done = bf16[1024,1025]{0,1:T(8,128)(2,1)} async-done(((bf16[512,1025]{0,1:T(8,128)(2,1)}), bf16[1024,1025]{0,1:T(8,128)(2,1)}) %all-gather.2.cloned.1.call-update) | async-done | bytes 2099216 | tf_op jit(solution)/shard_map/all_gather | solution.py:19
  31.1 3.4 %slice_bitcast_fusion.2 = (bf16[1024,1024]{1,0:T(8,128)(2,1)S(1)}, bf16[1024,1024]{0,1:T(8,128)(2,1)}) fusion(bf16[1024,1025]{0,1:T(8,128)(2,1)} %all-gather.2.cloned.1.call-done), kind=kLoop, calls=%fused_computation.76 | loop fusion | bytes 6291456 | tf_op jit(solution)/shard_map/transpose | solution.py:96
  34.5 3.9 %copy.20 = bf16[1024,1024]{1,0:T(8,128)(2,1)} copy(bf16[1024,1024]{0,1:T(8,128)(2,1)} %get-tuple-element.610) | data formatting | bytes 4194304
  38.5 1.4 fusion.37
  39.8 1.3 fusion.36
  41.1 17.6 %while.84 = (s32[]{:T(128)}, bf16[4,1024]{1,0:T(4,128)(2,1)S(1)}, f32[8,4,1024]{2,1,0:T(4,128)S(1)}, s32[8,4]{1,0:T(8,128)S(1)}, f32[1024]{0:T(1024)S(1)}, /*index=5*/bf16[1024,1024]{1,0:T(8,128)(2,1)}, s32[]{:T(128)}, s32[]{:T(128)}) while((s32[]{:T(128)}, bf16[4,1024]{1,0:T(4,128)(2,1)S(1)}, f32[8,4,1024]{2,1,0:T(4,128)S(1)}, ...), condition=%wide.region_5.6_spmd.clone, body=%wide.region_3.5_spmd.clone.sunk | while | flops 8413187 | bytes 2166943 | solution.py:59
  41.2 2.1 %fusion.79 = (f32[4]{0:T(128)S(1)}, f32[4,1024]{1,0:T(4,128)S(1)}) fusion(bf16[1024,1024]{1,0:T(8,128)(2,1)} %get-tuple-element.886, bf16[4,1024]{1,0:T(4,128)(2,1)S(1)} %get-tuple-element.874, pred[]{:T(512)S(6)} %compare.6, f32[1024]{0:T(1024)S(1)} %get-tuple-element.885, pred[4]{0:T(512)(128)(4,1)S(1)} %compare_bitcast_fusion.16, ...), kind=kOutput, calls=%fused_computation.80.clone.1 | convolution fusion | flops 8404988 | bytes 2142233 | tf_op jit(solution)/shard_map/while/body/eval_jaxpr/dot_general | solution.py:50
  43.4 2.1 %fusion.79 = (f32[4]{0:T(128)S(1)}, f32[4,1024]{1,0:T(4,128)S(1)}) fusion(bf16[1024,1024]{1,0:T(8,128)(2,1)} %get-tuple-element.886, bf16[4,1024]{1,0:T(4,128)(2,1)S(1)} %get-tuple-element.874, pred[]{:T(512)S(6)} %compare.6, f32[1024]{0:T(1024)S(1)} %get-tuple-element.885, pred[4]{0:T(512)(128)(4,1)S(1)} %compare_bitcast_fusion.16, ...), kind=kOutput, calls=%fused_computation.80.clone.1 | convolution fusion | flops 8404988 | bytes 2142233 | tf_op jit(solution)/shard_map/while/body/eval_jaxpr/dot_general | solution.py:50
  45.6 2.1 %fusion.79 = (f32[4]{0:T(128)S(1)}, f32[4,1024]{1,0:T(4,128)S(1)}) fusion(bf16[1024,1024]{1,0:T(8,128)(2,1)} %get-tuple-element.886, bf16[4,1024]{1,0:T(4,128)(2,1)S(1)} %get-tuple-element.874, pred[]{:T(512)S(6)} %compare.6, f32[1024]{0:T(1024)S(1)} %get-tuple-element.885, pred[4]{0:T(512)(128)(4,1)S(1)} %compare_bitcast_fusion.16, ...), kind=kOutput, calls=%fused_computation.80.clone.1 | convolution fusion | flops 8404988 | bytes 2142233 | tf_op jit(solution)/shard_map/while/body/eval_jaxpr/dot_general | solution.py:50
  47.8 2.1 %fusion.79 = (f32[4]{0:T(128)S(1)}, f32[4,1024]{1,0:T(4,128)S(1)}) fusion(bf16[1024,1024]{1,0:T(8,128)(2,1)} %get-tuple-element.886, bf16[4,1024]{1,0:T(4,128)(2,1)S(1)} %get-tuple-element.874, pred[]{:T(512)S(6)} %compare.6, f32[1024]{0:T(1024)S(1)} %get-tuple-element.885, pred[4]{0:T(512)(128)(4,1)S(1)} %compare_bitcast_fusion.16, ...), kind=kOutput, calls=%fused_computation.80.clone.1 | convolution fusion | flops 8404988 | bytes 2142233 | tf_op jit(solution)/shard_map/while/body/eval_jaxpr/dot_general | solution.py:50
  50.0 2.1 %fusion.79 = (f32[4]{0:T(128)S(1)}, f32[4,1024]{1,0:T(4,128)S(1)}) fusion(bf16[1024,1024]{1,0:T(8,128)(2,1)} %get-tuple-element.886, bf16[4,1024]{1,0:T(4,128)(2,1)S(1)} %get-tuple-element.874, pred[]{:T(512)S(6)} %compare.6, f32[1024]{0:T(1024)S(1)} %get-tuple-element.885, pred[4]{0:T(512)(128)(4,1)S(1)} %compare_bitcast_fusion.16, ...), kind=kOutput, calls=%fused_computation.80.clone.1 | convolution fusion | flops 8404988 | bytes 2142233 | tf_op jit(solution)/shard_map/while/body/eval_jaxpr/dot_general | solution.py:50
  52.2 2.1 %fusion.79 = (f32[4]{0:T(128)S(1)}, f32[4,1024]{1,0:T(4,128)S(1)}) fusion(bf16[1024,1024]{1,0:T(8,128)(2,1)} %get-tuple-element.886, bf16[4,1024]{1,0:T(4,128)(2,1)S(1)} %get-tuple-element.874, pred[]{:T(512)S(6)} %compare.6, f32[1024]{0:T(1024)S(1)} %get-tuple-element.885, pred[4]{0:T(512)(128)(4,1)S(1)} %compare_bitcast_fusion.16, ...), kind=kOutput, calls=%fused_computation.80.clone.1 | convolution fusion | flops 8404988 | bytes 2142233 | tf_op jit(solution)/shard_map/while/body/eval_jaxpr/dot_general | solution.py:50
  54.4 2.1 %fusion.79 = (f32[4]{0:T(128)S(1)}, f32[4,1024]{1,0:T(4,128)S(1)}) fusion(bf16[1024,1024]{1,0:T(8,128)(2,1)} %get-tuple-element.886, bf16[4,1024]{1,0:T(4,128)(2,1)S(1)} %get-tuple-element.874, pred[]{:T(512)S(6)} %compare.6, f32[1024]{0:T(1024)S(1)} %get-tuple-element.885, pred[4]{0:T(512)(128)(4,1)S(1)} %compare_bitcast_fusion.16, ...), kind=kOutput, calls=%fused_computation.80.clone.1 | convolution fusion | flops 8404988 | bytes 2142233 | tf_op jit(solution)/shard_map/while/body/eval_jaxpr/dot_general | solution.py:50
  56.6 2.1 %fusion.79 = (f32[4]{0:T(128)S(1)}, f32[4,1024]{1,0:T(4,128)S(1)}) fusion(bf16[1024,1024]{1,0:T(8,128)(2,1)} %get-tuple-element.886, bf16[4,1024]{1,0:T(4,128)(2,1)S(1)} %get-tuple-element.874, pred[]{:T(512)S(6)} %compare.6, f32[1024]{0:T(1024)S(1)} %get-tuple-element.885, pred[4]{0:T(512)(128)(4,1)S(1)} %compare_bitcast_fusion.16, ...), kind=kOutput, calls=%fused_computation.80.clone.1 | convolution fusion | flops 8404988 | bytes 2142233 | tf_op jit(solution)/shard_map/while/body/eval_jaxpr/dot_general | solution.py:50
  58.7 3.2 %collective-permute-start = (bf16[4,1024]{1,0:T(4,128)(2,1)S(1)}, bf16[4,1024]{1,0:T(4,128)(2,1)S(1)}, u32[]{:S(2)}, u32[]{:S(2)}) collective-permute-start(bf16[4,1024]{1,0:T(4,128)(2,1)S(1)} %get-tuple-element.437), channel_id=1, source_target_pairs={{0,1},{1,2},{2,3},{3,4},{4,5},{5,6},{6,7},{7,8},{8,9},{9,10},{10,1... | collective-permute-start | bytes 24584 | tf_op jit(solution)/shard_map/ppermute | solution.py:30
  61.9 4.8 %while.85 = (s32[]{:T(128)}, f32[4,1024]{1,0:T(4,128)S(1)}, s32[8,4]{1,0:T(8,128)S(1)}, f32[8,4,1024]{2,1,0:T(4,128)S(1)}, bf16[1024,1024]{1,0:T(8,128)(2,1)S(1)}, /*index=5*/s32[]{:T(128)}, s32[]{:T(128)}, s32[]{:T(128)}) while((s32[]{:T(128)}, f32[4,1024]{1,0:T(4,128)S(1)}, s32[8,4]{1,0:T(8,128)S(1)}, ...), condition=%wide.region_14.15_spmd.clone, body=%wide.region_12.14_spmd.clone.sunk | while | flops 8413188 | bytes 2179243 | solution.py:72
  62.0 0.5 fusion.81
  62.6 0.5 fusion.81
  63.1 0.5 fusion.81
  63.7 0.5 fusion.81
  64.3 0.5 fusion.81
  64.9 0.5 fusion.81
  65.5 0.5 fusion.81
  66.1 0.5 fusion.81
  66.7 1.9 %collective-permute-start.2 = (f32[4,1024]{1,0:T(4,128)S(1)}, f32[4,1024]{1,0:T(4,128)S(1)}, u32[]{:S(2)}, u32[]{:S(2)}) collective-permute-start(f32[4,1024]{1,0:T(4,128)S(1)} %get-tuple-element.440), channel_id=1, source_target_pairs={{1,0},{2,1},{3,2},{4,3},{5,4},{6,5},{7,6},{8,7},{9,8},{10,9},{11,1... | collective-permute-start | bytes 49160 | tf_op jit(solution)/shard_map/ppermute | solution.py:30
  68.6 17.6 %while.80 = (s32[]{:T(128)}, bf16[4,1024]{1,0:T(4,128)(2,1)S(1)}, f32[8,4,1024]{2,1,0:T(4,128)S(1)}, s32[8,4]{1,0:T(8,128)S(1)}, f32[1024]{0:T(1024)S(1)}, /*index=5*/bf16[1024,1024]{1,0:T(8,128)(2,1)}, s32[]{:T(128)}) while((s32[]{:T(128)}, bf16[4,1024]{1,0:T(4,128)(2,1)S(1)}, f32[8,4,1024]{2,1,0:T(4,128)S(1)}, s32[8,4]{1,0:T(8,128)S(1)}, ...), condition=%wide.region_8.9_spmd, body=%wide.region_6.8_spmd.sunk | while | flops 8409090 | bytes 2166925 | solution.py:59
  68.7 2.1 %fusion.70 = (f32[4]{0:T(128)S(1)}, f32[4,1024]{1,0:T(4,128)S(1)}) fusion(bf16[1024,1024]{1,0:T(8,128)(2,1)} %get-tuple-element.908, bf16[4,1024]{1,0:T(4,128)(2,1)S(1)} %get-tuple-element.897, f32[1024]{0:T(1024)S(1)} %get-tuple-element.907, pred[4]{0:T(512)(128)(4,1)S(1)} %compare_bitcast_fusion.12, f32[8,4,1024]{2,1,0:T(4,128)S(1)} %get-tuple-element.905, ...), kind=kOutput, calls=%fused_computation.77.clone.1 | convolution fusion | flops 8400892 | bytes 2142232 | tf_op jit(solution)/shard_map/while/body/eval_jaxpr/dot_general | solution.py:50
  70.9 2.1 %fusion.70 = (f32[4]{0:T(128)S(1)}, f32[4,1024]{1,0:T(4,128)S(1)}) fusion(bf16[1024,1024]{1,0:T(8,128)(2,1)} %get-tuple-element.908, bf16[4,1024]{1,0:T(4,128)(2,1)S(1)} %get-tuple-element.897, f32[1024]{0:T(1024)S(1)} %get-tuple-element.907, pred[4]{0:T(512)(128)(4,1)S(1)} %compare_bitcast_fusion.12, f32[8,4,1024]{2,1,0:T(4,128)S(1)} %get-tuple-element.905, ...), kind=kOutput, calls=%fused_computation.77.clone.1 | convolution fusion | flops 8400892 | bytes 2142232 | tf_op jit(solution)/shard_map/while/body/eval_jaxpr/dot_general | solution.py:50
  73.1 2.1 %fusion.70 = (f32[4]{0:T(128)S(1)}, f32[4,1024]{1,0:T(4,128)S(1)}) fusion(bf16[1024,1024]{1,0:T(8,128)(2,1)} %get-tuple-element.908, bf16[4,1024]{1,0:T(4,128)(2,1)S(1)} %get-tuple-element.897, f32[1024]{0:T(1024)S(1)} %get-tuple-element.907, pred[4]{0:T(512)(128)(4,1)S(1)} %compare_bitcast_fusion.12, f32[8,4,1024]{2,1,0:T(4,128)S(1)} %get-tuple-element.905, ...), kind=kOutput, calls=%fused_computation.77.clone.1 | convolution fusion | flops 8400892 | bytes 2142232 | tf_op jit(solution)/shard_map/while/body/eval_jaxpr/dot_general | solution.py:50
  75.3 2.1 %fusion.70 = (f32[4]{0:T(128)S(1)}, f32[4,1024]{1,0:T(4,128)S(1)}) fusion(bf16[1024,1024]{1,0:T(8,128)(2,1)} %get-tuple-element.908, bf16[4,1024]{1,0:T(4,128)(2,1)S(1)} %get-tuple-element.897, f32[1024]{0:T(1024)S(1)} %get-tuple-element.907, pred[4]{0:T(512)(128)(4,1)S(1)} %compare_bitcast_fusion.12, f32[8,4,1024]{2,1,0:T(4,128)S(1)} %get-tuple-element.905, ...), kind=kOutput, calls=%fused_computation.77.clone.1 | convolution fusion | flops 8400892 | bytes 2142232 | tf_op jit(solution)/shard_map/while/body/eval_jaxpr/dot_general | solution.py:50
  77.5 2.1 %fusion.70 = (f32[4]{0:T(128)S(1)}, f32[4,1024]{1,0:T(4,128)S(1)}) fusion(bf16[1024,1024]{1,0:T(8,128)(2,1)} %get-tuple-element.908, bf16[4,1024]{1,0:T(4,128)(2,1)S(1)} %get-tuple-element.897, f32[1024]{0:T(1024)S(1)} %get-tuple-element.907, pred[4]{0:T(512)(128)(4,1)S(1)} %compare_bitcast_fusion.12, f32[8,4,1024]{2,1,0:T(4,128)S(1)} %get-tuple-element.905, ...), kind=kOutput, calls=%fused_computation.77.clone.1 | convolution fusion | flops 8400892 | bytes 2142232 | tf_op jit(solution)/shard_map/while/body/eval_jaxpr/dot_general | solution.py:50
  79.7 2.1 %fusion.70 = (f32[4]{0:T(128)S(1)}, f32[4,1024]{1,0:T(4,128)S(1)}) fusion(bf16[1024,1024]{1,0:T(8,128)(2,1)} %get-tuple-element.908, bf16[4,1024]{1,0:T(4,128)(2,1)S(1)} %get-tuple-element.897, f32[1024]{0:T(1024)S(1)} %get-tuple-element.907, pred[4]{0:T(512)(128)(4,1)S(1)} %compare_bitcast_fusion.12, f32[8,4,1024]{2,1,0:T(4,128)S(1)} %get-tuple-element.905, ...), kind=kOutput, calls=%fused_computation.77.clone.1 | convolution fusion | flops 8400892 | bytes 2142232 | tf_op jit(solution)/shard_map/while/body/eval_jaxpr/dot_general | solution.py:50
  81.9 2.1 %fusion.70 = (f32[4]{0:T(128)S(1)}, f32[4,1024]{1,0:T(4,128)S(1)}) fusion(bf16[1024,1024]{1,0:T(8,128)(2,1)} %get-tuple-element.908, bf16[4,1024]{1,0:T(4,128)(2,1)S(1)} %get-tuple-element.897, f32[1024]{0:T(1024)S(1)} %get-tuple-element.907, pred[4]{0:T(512)(128)(4,1)S(1)} %compare_bitcast_fusion.12, f32[8,4,1024]{2,1,0:T(4,128)S(1)} %get-tuple-element.905, ...), kind=kOutput, calls=%fused_computation.77.clone.1 | convolution fusion | flops 8400892 | bytes 2142232 | tf_op jit(solution)/shard_map/while/body/eval_jaxpr/dot_general | solution.py:50
  84.0 2.1 %fusion.70 = (f32[4]{0:T(128)S(1)}, f32[4,1024]{1,0:T(4,128)S(1)}) fusion(bf16[1024,1024]{1,0:T(8,128)(2,1)} %get-tuple-element.908, bf16[4,1024]{1,0:T(4,128)(2,1)S(1)} %get-tuple-element.897, f32[1024]{0:T(1024)S(1)} %get-tuple-element.907, pred[4]{0:T(512)(128)(4,1)S(1)} %compare_bitcast_fusion.12, f32[8,4,1024]{2,1,0:T(4,128)S(1)} %get-tuple-element.905, ...), kind=kOutput, calls=%fused_computation.77.clone.1 | convolution fusion | flops 8400892 | bytes 2142232 | tf_op jit(solution)/shard_map/while/body/eval_jaxpr/dot_general | solution.py:50
  86.2 3.6 %collective-permute-start.1 = (bf16[4,1024]{1,0:T(4,128)(2,1)S(1)}, bf16[4,1024]{1,0:T(4,128)(2,1)S(1)}, u32[]{:S(2)}, u32[]{:S(2)}) collective-permute-start(bf16[4,1024]{1,0:T(4,128)(2,1)S(1)} %get-tuple-element.438), channel_id=1, source_target_pairs={{0,1},{1,2},{2,3},{3,4},{4,5},{5,6},{6,7},{7,8},{8,9},{9,10},{10,1... | collective-permute-start | bytes 24584 | tf_op jit(solution)/shard_map/ppermute | solution.py:30
  89.9 4.8 %while.82 = (s32[]{:T(128)}, f32[4,1024]{1,0:T(4,128)S(1)}, s32[8,4]{1,0:T(8,128)S(1)}, f32[8,4,1024]{2,1,0:T(4,128)S(1)}, bf16[1024,1024]{1,0:T(8,128)(2,1)S(1)}, /*index=5*/s32[]{:T(128)}, s32[]{:T(128)}) while((s32[]{:T(128)}, f32[4,1024]{1,0:T(4,128)S(1)}, s32[8,4]{1,0:T(8,128)S(1)}, f32[8,4,1024]{2,1,0:T(4,128)S(1)}, ...), condition=%wide.region_17.18_spmd, body=%wide.region_15.17_spmd.sunk | while | flops 8409091 | bytes 2179225 | solution.py:72
  89.9 0.5 fusion.75
  90.5 0.5 fusion.75
  91.1 0.5 fusion.75
  91.7 0.5 fusion.75
  92.3 0.5 fusion.75
  92.9 0.5 fusion.75
  94.1 0.5 fusion.75
  94.7 6.3 %collective-permute-start.3 = (f32[4,1024]{1,0:T(4,128)S(1)}, f32[4,1024]{1,0:T(4,128)S(1)}, u32[]{:S(2)}, u32[]{:S(2)}) collective-permute-start(f32[4,1024]{1,0:T(4,128)S(1)} %get-tuple-element.441), channel_id=1, source_target_pairs={{1,0},{2,1},{3,2},{4,3},{5,4},{6,5},{7,6},{8,7},{9,8},{10,9},{11,1... | collective-permute-start | bytes 49160 | tf_op jit(solution)/shard_map/ppermute | solution.py:30
  101.0 18.1 %while.81 = (s32[]{:T(128)}, bf16[4,1024]{1,0:T(4,128)(2,1)S(1)}, f32[8,4,1024]{2,1,0:T(4,128)S(1)}, f32[8,4]{1,0:T(8,128)S(1)}, f32[8,4,1024]{2,1,0:T(4,128)S(1...) while((s32[]{:T(128)}, bf16[4,1024]{1,0:T(4,128)(2,1)S(1)}, ...), condition=%wide.region_11.12_spmd, body=%wide.region_9.11_spmd.sunk | while | flops 8409090 | bytes 2183901 | solution.py:59
  101.0 2.1 %fusion.73 = (f32[4]{0:T(128)S(1)}, f32[4,1024]{1,0:T(4,128)S(1)}) fusion(bf16[1024,1024]{1,0:T(8,128)(2,1)} %get-tuple-element.937, bf16[4,1024]{1,0:T(4,128)(2,1)S(1)} %get-tuple-element.921, f32[1024]{0:T(1024)S(1)} %get-tuple-element.936, pred[4]{0:T(512)(128)(4,1)S(1)} %compare_bitcast_fusion.13, f32[8,4,1024]{2,1,0:T(4,128)S(1)} %get-tuple-element.934, ...), kind=kOutput, calls=%fused_computation.82.clone.1 | convolution fusion | flops 8400892 | bytes 2142232 | tf_op jit(solution)/shard_map/while/body/eval_jaxpr/dot_general | solution.py:50
  103.3 2.1 %fusion.73 = (f32[4]{0:T(128)S(1)}, f32[4,1024]{1,0:T(4,128)S(1)}) fusion(bf16[1024,1024]{1,0:T(8,128)(2,1)} %get-tuple-element.937, bf16[4,1024]{1,0:T(4,128)(2,1)S(1)} %get-tuple-element.921, f32[1024]{0:T(1024)S(1)} %get-tuple-element.936, pred[4]{0:T(512)(128)(4,1)S(1)} %compare_bitcast_fusion.13, f32[8,4,1024]{2,1,0:T(4,128)S(1)} %get-tuple-element.934, ...), kind=kOutput, calls=%fused_computation.82.clone.1 | convolution fusion | flops 8400892 | bytes 2142232 | tf_op jit(solution)/shard_map/while/body/eval_jaxpr/dot_general | solution.py:50
  105.5 2.1 %fusion.73 = (f32[4]{0:T(128)S(1)}, f32[4,1024]{1,0:T(4,128)S(1)}) fusion(bf16[1024,1024]{1,0:T(8,128)(2,1)} %get-tuple-element.937, bf16[4,1024]{1,0:T(4,128)(2,1)S(1)} %get-tuple-element.921, f32[1024]{0:T(1024)S(1)} %get-tuple-element.936, pred[4]{0:T(512)(128)(4,1)S(1)} %compare_bitcast_fusion.13, f32[8,4,1024]{2,1,0:T(4,128)S(1)} %get-tuple-element.934, ...), kind=kOutput, calls=%fused_computation.82.clone.1 | convolution fusion | flops 8400892 | bytes 2142232 | tf_op jit(solution)/shard_map/while/body/eval_jaxpr/dot_general | solution.py:50
  107.8 2.1 %fusion.73 = (f32[4]{0:T(128)S(1)}, f32[4,1024]{1,0:T(4,128)S(1)}) fusion(bf16[1024,1024]{1,0:T(8,128)(2,1)} %get-tuple-element.937, bf16[4,1024]{1,0:T(4,128)(2,1)S(1)} %get-tuple-element.921, f32[1024]{0:T(1024)S(1)} %get-tuple-element.936, pred[4]{0:T(512)(128)(4,1)S(1)} %compare_bitcast_fusion.13, f32[8,4,1024]{2,1,0:T(4,128)S(1)} %get-tuple-element.934, ...), kind=kOutput, calls=%fused_computation.82.clone.1 | convolution fusion | flops 8400892 | bytes 2142232 | tf_op jit(solution)/shard_map/while/body/eval_jaxpr/dot_general | solution.py:50
  110.1 2.1 %fusion.73 = (f32[4]{0:T(128)S(1)}, f32[4,1024]{1,0:T(4,128)S(1)}) fusion(bf16[1024,1024]{1,0:T(8,128)(2,1)} %get-tuple-element.937, bf16[4,1024]{1,0:T(4,128)(2,1)S(1)} %get-tuple-element.921, f32[1024]{0:T(1024)S(1)} %get-tuple-element.936, pred[4]{0:T(512)(128)(4,1)S(1)} %compare_bitcast_fusion.13, f32[8,4,1024]{2,1,0:T(4,128)S(1)} %get-tuple-element.934, ...), kind=kOutput, calls=%fused_computation.82.clone.1 | convolution fusion | flops 8400892 | bytes 2142232 | tf_op jit(solution)/shard_map/while/body/eval_jaxpr/dot_general | solution.py:50
  112.3 2.1 %fusion.73 = (f32[4]{0:T(128)S(1)}, f32[4,1024]{1,0:T(4,128)S(1)}) fusion(bf16[1024,1024]{1,0:T(8,128)(2,1)} %get-tuple-element.937, bf16[4,1024]{1,0:T(4,128)(2,1)S(1)} %get-tuple-element.921, f32[1024]{0:T(1024)S(1)} %get-tuple-element.936, pred[4]{0:T(512)(128)(4,1)S(1)} %compare_bitcast_fusion.13, f32[8,4,1024]{2,1,0:T(4,128)S(1)} %get-tuple-element.934, ...), kind=kOutput, calls=%fused_computation.82.clone.1 | convolution fusion | flops 8400892 | bytes 2142232 | tf_op jit(solution)/shard_map/while/body/eval_jaxpr/dot_general | solution.py:50
  114.6 2.1 %fusion.73 = (f32[4]{0:T(128)S(1)}, f32[4,1024]{1,0:T(4,128)S(1)}) fusion(bf16[1024,1024]{1,0:T(8,128)(2,1)} %get-tuple-element.937, bf16[4,1024]{1,0:T(4,128)(2,1)S(1)} %get-tuple-element.921, f32[1024]{0:T(1024)S(1)} %get-tuple-element.936, pred[4]{0:T(512)(128)(4,1)S(1)} %compare_bitcast_fusion.13, f32[8,4,1024]{2,1,0:T(4,128)S(1)} %get-tuple-element.934, ...), kind=kOutput, calls=%fused_computation.82.clone.1 | convolution fusion | flops 8400892 | bytes 2142232 | tf_op jit(solution)/shard_map/while/body/eval_jaxpr/dot_general | solution.py:50
  116.8 2.1 %fusion.73 = (f32[4]{0:T(128)S(1)}, f32[4,1024]{1,0:T(4,128)S(1)}) fusion(bf16[1024,1024]{1,0:T(8,128)(2,1)} %get-tuple-element.937, bf16[4,1024]{1,0:T(4,128)(2,1)S(1)} %get-tuple-element.921, f32[1024]{0:T(1024)S(1)} %get-tuple-element.936, pred[4]{0:T(512)(128)(4,1)S(1)} %compare_bitcast_fusion.13, f32[8,4,1024]{2,1,0:T(4,128)S(1)} %get-tuple-element.934, ...), kind=kOutput, calls=%fused_computation.82.clone.1 | convolution fusion | flops 8400892 | bytes 2142232 | tf_op jit(solution)/shard_map/while/body/eval_jaxpr/dot_general | solution.py:50
  119.1 0.7 copy.24
  119.8 4.9 %while.83 = (s32[]{:T(128)}, f32[4,1024]{1,0:T(4,128)S(1)}, f32[8,4,1024]{2,1,0:T(4,128)S(1)}, s32[8,4]{1,0:T(8,128)S(1)}, f32[8,4,1024]{2,1,0:T(4,128)S(1)}, /*...) while((s32[]{:T(128)}, f32[4,1024]{1,0:T(4,128)S(1)}, f32[8,4,1024]{2,1,0:T(4,128)S(1)}, ...), condition=%wide.region_20.21_spmd, body=%wide.region_18.20_spmd.sunk | while | flops 8409091 | bytes 2212005 | solution.py:72
  124.9 10.6 %all_to_all.23 = bf16[2,4,8,512]{3,1,2,0:T(4,128)(2,1)S(1)} all-to-all(bf16[2,4,8,512]{3,1,2,0:T(4,128)(2,1)S(1)} %pad_maximum_fusion.1), channel_id=1, replica_groups=mesh['tm'=256,'state'=2] {'state'}, dimensions={0} | all-to-all | bytes 131072 | tf_op jit(solution)/shard_map/all_to_all | solution.py:12
  135.5 0.6 copy.28
  (163 shorter events, 11.1 us)
Async XLA Ops:
  7.2 10.8 %copy-start = (s32[4,16]{1,0:T(4,128)S(1)}, s32[4,16]{1,0:T(4,128)}, u32[]{:S(2)}) copy-start(s32[4,16]{1,0:T(4,128)} %param.23) | copy-start | bytes 772
  7.2 1.6 %copy-start.4 = (bf16[512]{0:T(512)(128)(2,1)S(1)}, bf16[512]{0:T(512)(128)(2,1)}, u32[]{:S(2)}) copy-start(bf16[512]{0:T(512)(128)(2,1)} %param.22) | copy-start | bytes 3076
  7.2 23.9 %all-gather.2.cloned.1.call-start = ((), (), s32[]{:S(2)}) async-start(), calls=%async_computation.2 | async-start | bytes 3170304 | tf_op jit(solution)/shard_map/all_gather | solution.py:19
  8.8 1.6 %copy-start.1 = (f32[512,512]{1,0:T(8,128)S(1)}, f32[512,512]{1,0:T(8,128)}, u32[]{:S(2)}) copy-start(f32[512,512]{1,0:T(8,128)} %param.20) | copy-start | bytes 3145732
  8.8 1.9 %copy-start.2 = (f32[512,512]{1,0:T(8,128)S(1)}, f32[512,512]{1,0:T(8,128)}, u32[]{:S(2)}) copy-start(f32[512,512]{1,0:T(8,128)} %param.19) | copy-start | bytes 3145732
  9.9 1.1 copy-start.3
  14.0 5.2 %all-to-all-start = ((f32[4,16,512]{2,0,1:T(4,128)}), f32[4,16,512]{2,0,1:T(4,128)S(1)}, u32[]{:S(2)}, u32[]{:S(2)}) async-start(f32[4,16,512]{2,0,1:T(4,128)} %copy.16), calls=%async_computation | async-start | bytes 262144 | tf_op jit(solution)/shard_map/all_to_all | solution.py:114
  58.7 9.9 %collective-permute-start = (bf16[4,1024]{1,0:T(4,128)(2,1)S(1)}, bf16[4,1024]{1,0:T(4,128)(2,1)S(1)}, u32[]{:S(2)}, u32[]{:S(2)}) collective-permute-start(bf16[4,1024]{1,0:T(4,128)(2,1)S(1)} %get-tuple-element.437), channel_id=1, source_target_pairs={{0,1},{1,2},{2,3},{3,4},{4,5},{5,6},{6,7},{7,8},{8,9},{9,10},{10,1... | collective-permute-start | bytes 24584 | tf_op jit(solution)/shard_map/ppermute | solution.py:30
  66.7 23.2 %collective-permute-start.2 = (f32[4,1024]{1,0:T(4,128)S(1)}, f32[4,1024]{1,0:T(4,128)S(1)}, u32[]{:S(2)}, u32[]{:S(2)}) collective-permute-start(f32[4,1024]{1,0:T(4,128)S(1)} %get-tuple-element.440), channel_id=1, source_target_pairs={{1,0},{2,1},{3,2},{4,3},{5,4},{6,5},{7,6},{8,7},{9,8},{10,9},{11,1... | collective-permute-start | bytes 49160 | tf_op jit(solution)/shard_map/ppermute | solution.py:30
  86.2 14.7 %collective-permute-start.1 = (bf16[4,1024]{1,0:T(4,128)(2,1)S(1)}, bf16[4,1024]{1,0:T(4,128)(2,1)S(1)}, u32[]{:S(2)}, u32[]{:S(2)}) collective-permute-start(bf16[4,1024]{1,0:T(4,128)(2,1)S(1)} %get-tuple-element.438), channel_id=1, source_target_pairs={{0,1},{1,2},{2,3},{3,4},{4,5},{5,6},{6,7},{7,8},{8,9},{9,10},{10,1... | collective-permute-start | bytes 24584 | tf_op jit(solution)/shard_map/ppermute | solution.py:30
  94.7 25.1 %collective-permute-start.3 = (f32[4,1024]{1,0:T(4,128)S(1)}, f32[4,1024]{1,0:T(4,128)S(1)}, u32[]{:S(2)}, u32[]{:S(2)}) collective-permute-start(f32[4,1024]{1,0:T(4,128)S(1)} %get-tuple-element.441), channel_id=1, source_target_pairs={{1,0},{2,1},{3,2},{4,3},{5,4},{6,5},{7,6},{8,7},{9,8},{10,9},{11,1... | collective-permute-start | bytes 49160 | tf_op jit(solution)/shard_map/ppermute | solution.py:30
Sparse Core Ops, SparseCore 0:
  10.1 20.9 all-gather.1
